TPU v7x, 512 devices: a whole 4x4x16 slice. The times are simulated.
512 devices in a mesh: sta: 16 (over x_lo, y, core), src: 32 (over z, x_hi).
Axes of the slice: x: 4 (x_hi: 2, x_lo: 2; x = x_hi * 2 + x_lo), y: 4, z: 16, core: 2. Of those that a mesh axis runs over, the one named last changes fastest.
Arguments:
- features: bfloat16 [512, 1024, 128], P('sta', 'src'), may hold values from -6 to 6
- station_lists: int32 [512, 16], replicated, may hold values from 0 to 511, as said below
- station_counts: int32 [512], replicated, may hold values from 1 to 16
- source_lists: int32 [1024, 16], replicated, may hold values from 0 to 1023, as said below
- source_counts: int32 [1024], replicated, may hold values from 1 to 16
- picks: int32 [2, 512], P(None, 'sta'), may hold values 0 or 1
- targets: float32 [2, 1024], P(None, 'src'), may hold values from 0 to 1
- layer_weights: bfloat16 [2, 3, 64, 64], replicated, may hold values from -0.75 to 0.75
- readout_vector: bfloat16 [64], replicated, may hold values from -0.75 to 0.75
Outputs:
- likelihood: float32 [2, 1024], P(None, 'src')
- feature_grad: bfloat16 [512, 1024, 128], P('sta', 'src')
- weight_grad: float32 [2, 3, 64, 64], replicated
- vector_grad: float32 [64], replicated
Inputs may be any that keep to these rules, and one draw needn't show every extreme that they name: `station_lists`: every entry of a station's list lies within 16 rows of that station; entries past its count are padding. `source_lists`: every entry of a source node's list lies within 16 rows of that source node; entries past its count are padding.
All inputs are finite; a program needn't handle non-finite values. No bound on the sum of `picks` on one device may be relied on, other than what follows from the above.
Results may differ from a plain program's by a relative error of at most 0.015.
Values may be sent and summed in bfloat16 or wider, within the bound.
No kernel may reach another device: no remote copies, remote signals or barrier semaphores. Data moves between devices by JAX's collectives and lax.ppermute only.
A program may use at most 64 MiB of HBM per device.

v0:
```python
import jax
import jax.numpy as jnp
from jax import lax
from jax.sharding import PartitionSpec as P

LAYERS = 2
HW = 16


def padded_2(cells, sides, width):
    for axis, dim in sides:
        count = lax.axis_size(axis)
        ends = count - 1
        head = lax.slice_in_dim(cells, 0, width, axis=dim)
        tail = lax.slice_in_dim(cells, cells.shape[dim] - width, cells.shape[dim], axis=dim)
        cells = jnp.concatenate(
            [
                lax.ppermute(tail, axis, [(i, (i + 1) % count) for i in range(ends)]),
                cells,
                lax.ppermute(head, axis, [((i + 1) % count, i) for i in range(ends)]),
            ],
            axis=dim,
        )
    return cells


def count_matrix(lists, counts, first_row, span):
    list_width = lists.shape[1]
    in_list = jnp.arange(list_width)[None, :] < counts[:, None]
    shifted = lists - first_row
    matches = (shifted[:, :, None] == jnp.arange(span)[None, None, :]) & in_list[:, :, None]
    return jnp.sum(matches.astype(jnp.float32), axis=1).astype(jnp.bfloat16)


def blocked(matrix, windows):
    return jnp.kron(jnp.eye(windows, dtype=jnp.bfloat16), matrix)


def apply_block(values, matrix):
    channels = values.shape[-1]
    flat = values.reshape(-1, channels)
    return jnp.dot(flat, matrix, preferred_element_type=jnp.float32).reshape(values.shape)


def outer_sum(left, right, feature):
    return jnp.einsum(
        "nf,ng->fg",
        left.reshape(-1, feature),
        right.reshape(-1, feature),
        preferred_element_type=jnp.float32,
    )


def shards(
    features,
    station_lists,
    station_counts,
    source_lists,
    source_counts,
    picks,
    targets,
    layer_weights,
    readout_vector,
):
    sta_rows, src_rows, channels = features.shape
    feature = layer_weights.shape[-1]
    windows = channels // feature
    sta_first = lax.axis_index("sta") * sta_rows
    src_first = lax.axis_index("src") * src_rows
    own_slists = lax.dynamic_slice_in_dim(station_lists, sta_first, sta_rows, 0)
    own_scounts = lax.dynamic_slice_in_dim(station_counts, sta_first, sta_rows, 0)
    own_rlists = lax.dynamic_slice_in_dim(source_lists, src_first, src_rows, 0)
    own_rcounts = lax.dynamic_slice_in_dim(source_counts, src_first, src_rows, 0)
    sta_mix = count_matrix(own_slists, own_scounts, sta_first - HW, sta_rows + 2 * HW)
    src_mix = count_matrix(own_rlists, own_rcounts, src_first - HW, src_rows + 2 * HW)
    sta_div = own_scounts.astype(jnp.float32)[:, None, None]
    src_div = own_rcounts.astype(jnp.float32)[None, :, None]
    blocks = [
        [blocked(layer_weights[layer_idx, which], windows) for which in range(3)]
        for layer_idx in range(LAYERS)
    ]
    states = features
    saved = []
    for layer_idx in range(LAYERS):
        padded = padded_2(states, (("sta", 0), ("src", 1)), HW)
        along_sta = jnp.einsum(
            "im,mjc->ijc",
            sta_mix,
            padded[:, HW : HW + src_rows],
            preferred_element_type=jnp.float32,
        )
        sta_mean = (along_sta / sta_div).astype(jnp.bfloat16)
        along_src = jnp.einsum(
            "jm,imc->ijc", src_mix, padded[HW : HW + sta_rows], preferred_element_type=jnp.float32
        )
        src_mean = (along_src / src_div).astype(jnp.bfloat16)
        linear = (
            apply_block(states, blocks[layer_idx][0])
            + apply_block(sta_mean, blocks[layer_idx][1])
            + apply_block(src_mean, blocks[layer_idx][2])
        )
        squashed = jnp.tanh(linear)
        saved.append((states, sta_mean, src_mean, squashed))
        states = (states.astype(jnp.float32) + squashed).astype(jnp.bfloat16)
    vector_cols = (
        jnp.eye(windows, dtype=jnp.bfloat16)[:, None, :] * readout_vector[None, :, None]
    ).reshape(channels, windows)
    score = jnp.dot(
        states.reshape(-1, channels), vector_cols, preferred_element_type=jnp.float32
    ).reshape(sta_rows, src_rows, windows)
    picked = picks.astype(jnp.float32)
    partial_sum = jnp.sum(picked.T[:, None, :] * score, axis=0).T
    local_count = jnp.sum(picked, axis=1)
    summed, count = lax.psum((partial_sum, local_count), "sta")
    root = jnp.sqrt(jnp.maximum(count, 1.0))
    likelihood = summed / root[:, None]
    error = jax.nn.sigmoid(likelihood) - targets
    d_score = (picked.T[:, None, :] * error.T[None, :, :]).astype(jnp.bfloat16)
    v_sum = jnp.einsum(
        "nw,nwf->f",
        d_score.reshape(-1, windows),
        states.reshape(-1, windows, feature),
        preferred_element_type=jnp.float32,
    )
    grad = (d_score.astype(jnp.float32)[..., None] * readout_vector.astype(jnp.float32)).reshape(
        sta_rows, src_rows, channels
    )
    w_rows = []
    for layer_idx in reversed(range(LAYERS)):
        before, sta_mean, src_mean, squashed = saved[layer_idx]
        delta = (grad * (1.0 - squashed * squashed)).astype(jnp.bfloat16)
        w_rows.append(
            jnp.stack(
                [
                    outer_sum(before, delta, feature),
                    outer_sum(sta_mean, delta, feature),
                    outer_sum(src_mean, delta, feature),
                ]
            )
        )
        u_sta = (apply_block(delta, blocks[layer_idx][1].T) / sta_div).astype(jnp.bfloat16)
        u_src = (apply_block(delta, blocks[layer_idx][2].T) / src_div).astype(jnp.bfloat16)
        direct = grad + apply_block(delta, blocks[layer_idx][0].T)
        spread_sta = jnp.einsum("im,ijc->mjc", sta_mix, u_sta, preferred_element_type=jnp.float32)
        rim_rows = jnp.concatenate([spread_sta[:HW], spread_sta[sta_rows + HW :]], 0)
        got_rows = padded_2(rim_rows.astype(jnp.bfloat16), (("sta", 0),), HW).astype(rim_rows.dtype)
        from_sta = spread_sta[HW : sta_rows + HW]
        from_sta = from_sta + jnp.pad(got_rows[:HW], ((0, sta_rows - HW), (0, 0), (0, 0)))
        from_sta = from_sta + jnp.pad(got_rows[3 * HW :], ((sta_rows - HW, 0), (0, 0), (0, 0)))
        spread_src = jnp.einsum("jm,ijc->imc", src_mix, u_src, preferred_element_type=jnp.float32)
        rim_cols = jnp.concatenate([spread_src[:, :HW], spread_src[:, src_rows + HW :]], 1)
        got_cols = padded_2(rim_cols.astype(jnp.bfloat16), (("src", 1),), HW).astype(rim_cols.dtype)
        from_src = spread_src[:, HW : src_rows + HW]
        from_src = from_src + jnp.pad(got_cols[:, :HW], ((0, 0), (0, src_rows - HW), (0, 0)))
        from_src = from_src + jnp.pad(got_cols[:, 3 * HW :], ((0, 0), (src_rows - HW, 0), (0, 0)))
        grad = direct + from_sta + from_src
    w_sum = jnp.stack(w_rows[::-1])
    w_total, v_total = lax.psum((w_sum, v_sum), ("sta", "src"))
    node_total = jnp.float32(sta_rows * lax.axis_size("sta")) * jnp.float32(
        src_rows * lax.axis_size("src")
    )
    factor = 1.0 / jnp.sqrt(node_total)
    return (likelihood, grad.astype(jnp.bfloat16), w_total * factor, v_total * factor)


def solution(mesh):
    in_specs = (P("sta", "src", None), P(), P(), P(), P(), P(None, "sta"), P(None, "src"), P(), P())
    out_specs = (P(None, "src"), P("sta", "src", None), P(), P())
    return jax.shard_map(shards, mesh=mesh, in_specs=in_specs, out_specs=out_specs, check_vma=False)
```

profile of v0, /device:TPU:1, one launch (start us, length us, event | category | flops | bytes accessed | tf_op | source)
XLA Modules:
  0.0 722.8 jit_solution(12138712805420795126)
XLA Ops:
  8.3 4.6 collective-permute-start
  12.9 5.5 collective-permute-start.1
  19.1 1.2 fusion.59
  20.5 1.3 fusion.60
  31.4 1.3 collective-permute-start.2
  32.7 1.3 collective-permute-start.3
  36.4 7.6 %collective-permute-done.2 = bf16[64,16,128]{2,0,1:T(8,128)(2,1)S(1)} collective-permute-done((bf16[64,16,128]{2,0,1:T(8,128)(2,1)S(1)}, bf16[64,16,128]{2,0,1:T(8,128)(2,1)S(1)}, u32[]{:S(2)}, u32[]{:S(2)}) %collective-permute-start.2) | collective-permute-done | bytes 262176 | tf_op jit(solution)/shard_map/ppermute | solution.py:18
  48.2 3.6 collective-permute-start.4
  51.8 1.9 collective-permute-start.5
  53.9 4.1 collective-permute-done.5
  58.2 5.6 collective-permute-start.6
  63.8 1.3 collective-permute-start.7
  65.5 1.1 reshape.268
  67.3 5.6 collective-permute-done.7
  74.5 1.1 reshape.270
  76.8 25.8 %all-reduce.4 = (f32[2,32]{1,0:T(2,128)S(1)}, f32[2]{0:T(128)S(1)}) all-reduce(f32[2,32]{1,0:T(2,128)S(1)} %bitcast.115, f32[2]{0:T(128)S(1)} %copy-done.40), channel_id=1, replica_groups=mesh['sta'=16,'src'=32] {'sta'}, use_global_device_ids=true, to_apply=%region_3.4 | all-reduce | flops 66 | bytes 528 | tf_op jit(solution)/shard_map/psum | solution.py:114
  104.9 1.2 mul.284
  108.7 1.4 copy.149
  110.7 2.4 fusion.69
  113.4 115.2 %psum.31 = f32[64]{0:T(128)S(1)} all-reduce(f32[64]{0:T(128)S(1)} %convolution_bitcast_fusion.9), channel_id=1, replica_groups=mesh['sta'=16,'src'=32] {'sta','src'}, use_global_device_ids=true, to_apply=%region_7.8 | all-reduce | flops 64 | bytes 512 | tf_op jit(solution)/shard_map/psum | solution.py:158
  231.3 2.9 collective-permute-start.8
  234.2 1.9 collective-permute-start.9
  236.2 3.5 collective-permute-start.10
  239.6 1.5 collective-permute-start.11
  242.2 5.4 collective-permute-done.11
  248.7 1.2 multiply_convert_fusion
  252.4 1.7 fusion.70
  257.7 4.3 collective-permute-start.12
  262.0 1.9 collective-permute-start.13
  264.0 4.2 collective-permute-start.14
  268.2 1.3 collective-permute-start.15
  269.5 442.2 %all-reduce.7.cloned.1.call-done = f32[2,3,64,64]{2,3,1,0:T(8,128)} async-done(((f32[2,3,64,64]{2,3,1,0:T(8,128)}), f32[2,3,64,64]{2,3,1,0:T(8,128)}) %all-reduce.7.cloned.1.call-update) | async-done | bytes 98320 | tf_op jit(solution)/shard_map/psum | solution.py:158
  (193 shorter events, 42.8 us)
Async XLA Ops:
  7.2 704.5 %all-reduce.7.cloned.1.call-start = ((), (), s32[]{:S(2)}) async-start(), calls=%async_computation | async-start | bytes 393216 | tf_op jit(solution)/shard_map/psum | solution.py:158
  8.3 22.9 %collective-permute-start = (bf16[16,32,128]{2,0,1:T(8,128)(2,1)S(1)}, bf16[16,32,128]{2,0,1:T(8,128)(2,1)S(1)}, u32[]{:S(2)}, u32[]{:S(2)}) collective-permute-start(bf16[16,32,128]{2,0,1:T(8,128)(2,1)S(1)} %copy.146), channel_id=1, source_target_pairs={{0,32},{32,64},{64,96},{96,128},{128,160},{160,192},{192,224},{224... | collective-permute-start | bytes 393224 | tf_op jit(solution)/shard_map/ppermute | solution.py:18
  12.9 9.9 %copy-start.19 = (bf16[2,3,64,64]{3,2,1,0:T(8,128)(2,1)S(1)}, bf16[2,3,64,64]{3,2,1,0:T(8,128)(2,1)}, u32[]{:S(2)}) copy-start(bf16[2,3,64,64]{3,2,1,0:T(8,128)(2,1)} %param.16) | copy-start | bytes 147460
  12.9 18.4 %collective-permute-start.1 = (bf16[16,32,128]{2,0,1:T(8,128)(2,1)S(1)}, bf16[16,32,128]{2,0,1:T(8,128)(2,1)S(1)}, u32[]{:S(2)}, u32[]{:S(2)}) collective-permute-start(bf16[16,32,128]{2,0,1:T(8,128)(2,1)S(1)} %copy.147), channel_id=1, source_target_pairs={{32,0},{64,32},{96,64},{128,96},{160,128},{192,160},{224,192},{256... | collective-permute-start | bytes 393224 | tf_op jit(solution)/shard_map/ppermute | solution.py:20
  19.1 56.8 %copy-start.20 = (f32[32,2]{0,1:T(2,128)}, f32[32,2]{0,1:T(2,128)S(1)}, u32[]{:S(2)}) copy-start(f32[32,2]{0,1:T(2,128)S(1)} %convert_bitcast_fusion) | copy-start | bytes 772
  22.7 1.5 copy-start
  24.2 40.9 %copy-start.22 = (bf16[32,64]{1,0:T(8,128)(2,1)}, bf16[32,64]{1,0:T(8,128)(2,1)S(1)}, u32[]{:S(2)}) copy-start(bf16[32,64]{1,0:T(8,128)(2,1)S(1)} %convert_reduce_fusion.1) | copy-start | bytes 12292
  31.4 12.6 %collective-permute-start.2 = (bf16[64,16,128]{2,0,1:T(8,128)(2,1)S(1)}, bf16[64,16,128]{2,0,1:T(8,128)(2,1)S(1)}, u32[]{:S(2)}, u32[]{:S(2)}) collective-permute-start(bf16[64,16,128]{2,0,1:T(8,128)(2,1)S(1)} %get-tuple-element.38), channel_id=1, source_target_pairs={{0,1},{1,2},{2,3},{3,4},{4,5},{5,6},{6,7},{7,8},{8,9},{9,10},{10,1... | collective-permute-start | bytes 786440 | tf_op jit(solution)/shard_map/ppermute | solution.py:18
  32.7 1.3 copy-start.36
  32.7 11.4 %collective-permute-start.3 = (bf16[64,16,128]{2,0,1:T(8,128)(2,1)S(1)}, bf16[64,16,128]{2,0,1:T(8,128)(2,1)S(1)}, u32[]{:S(2)}, u32[]{:S(2)}) collective-permute-start(bf16[64,16,128]{2,0,1:T(8,128)(2,1)S(1)} %get-tuple-element.39), channel_id=1, source_target_pairs={{1,0},{2,1},{3,2},{4,3},{5,4},{6,5},{7,6},{8,7},{9,8},{10,9},{11,1... | collective-permute-start | bytes 786440 | tf_op jit(solution)/shard_map/ppermute | solution.py:20
  36.4 7.8 %copy-start.25 = (bf16[32,64]{1,0:T(8,128)(2,1)S(1)}, bf16[32,64]{1,0:T(8,128)(2,1)}, u32[]{:S(2)}) copy-start(bf16[32,64]{1,0:T(8,128)(2,1)} %convert_reduce_fusion) | copy-start | bytes 12292
  48.2 5.7 collective-permute-start.4
  51.8 6.3 collective-permute-start.5
  58.2 6.9 copy-start.37
  58.2 9.1 %collective-permute-start.6 = (bf16[64,16,128]{2,1,0:T(8,128)(2,1)S(1)}, bf16[64,16,128]{2,1,0:T(8,128)(2,1)S(1)}, u32[]{:S(2)}, u32[]{:S(2)}) collective-permute-start(bf16[64,16,128]{2,1,0:T(8,128)(2,1)S(1)} %get-tuple-element.36), channel_id=1, source_target_pairs={{0,1},{1,2},{2,3},{3,4},{4,5},{5,6},{6,7},{7,8},{8,9},{9,10},{10,1... | collective-permute-start | bytes 786440 | tf_op jit(solution)/shard_map/ppermute | solution.py:18
  63.8 9.1 %collective-permute-start.7 = (bf16[64,16,128]{2,1,0:T(8,128)(2,1)S(1)}, bf16[64,16,128]{2,1,0:T(8,128)(2,1)S(1)}, u32[]{:S(2)}, u32[]{:S(2)}) collective-permute-start(bf16[64,16,128]{2,1,0:T(8,128)(2,1)S(1)} %get-tuple-element.37), channel_id=1, source_target_pairs={{1,0},{2,1},{3,2},{4,3},{5,4},{6,5},{7,6},{8,7},{9,8},{10,9},{11,1... | collective-permute-start | bytes 786440 | tf_op jit(solution)/shard_map/ppermute | solution.py:20
  66.6 6.3 copy-start.26
  110.7 2.5 copy-start.1
  113.1 116.0 %copy-start.7 = (bf16[2048,64]{1,0:T(8,128)(2,1)S(1)}, bf16[2048,64]{1,0:T(8,128)(2,1)}, u32[]{:S(2)}) copy-start(bf16[2048,64]{1,0:T(8,128)(2,1)} %reshape.269) | copy-start | bytes 786436
  230.2 5.9 copy-start.16
  231.2 9.9 %copy-start.5 = (bf16[2048,64]{1,0:T(8,128)(2,1)S(1)}, bf16[2048,64]{1,0:T(8,128)(2,1)}, u32[]{:S(2)}) copy-start(bf16[2048,64]{1,0:T(8,128)(2,1)} %reshape.266) | copy-start | bytes 786436
  231.3 10.8 %collective-permute-start.8 = (bf16[16,32,128]{2,1,0:T(8,128)(2,1)S(1)}, bf16[16,32,128]{2,1,0:T(8,128)(2,1)S(1)}, u32[]{:S(2)}, u32[]{:S(2)}) collective-permute-start(bf16[16,32,128]{2,1,0:T(8,128)(2,1)S(1)} %get-tuple-element.32), channel_id=1, source_target_pairs={{0,32},{32,64},{64,96},{96,128},{128,160},{160,192},{192,224},{224... | collective-permute-start | bytes 393224 | tf_op jit(solution)/shard_map/ppermute | solution.py:18
  234.2 7.9 %collective-permute-start.9 = (bf16[16,32,128]{2,1,0:T(8,128)(2,1)S(1)}, bf16[16,32,128]{2,1,0:T(8,128)(2,1)S(1)}, u32[]{:S(2)}, u32[]{:S(2)}) collective-permute-start(bf16[16,32,128]{2,1,0:T(8,128)(2,1)S(1)} %get-tuple-element.33), channel_id=1, source_target_pairs={{32,0},{64,32},{96,64},{128,96},{160,128},{192,160},{224,192},{256... | collective-permute-start | bytes 393224 | tf_op jit(solution)/shard_map/ppermute | solution.py:20
  236.2 6.0 collective-permute-start.10
  239.6 8.0 %collective-permute-start.11 = (bf16[32,16,128]{2,1,0:T(8,128)(2,1)S(1)}, bf16[32,16,128]{2,1,0:T(8,128)(2,1)S(1)}, u32[]{:S(2)}, u32[]{:S(2)}) collective-permute-start(bf16[32,16,128]{2,1,0:T(8,128)(2,1)S(1)} %get-tuple-element.35), channel_id=1, source_target_pairs={{1,0},{2,1},{3,2},{4,3},{5,4},{6,5},{7,6},{8,7},{9,8},{10,9},{11,1... | collective-permute-start | bytes 393224 | tf_op jit(solution)/shard_map/ppermute | solution.py:20
  242.2 5.6 copy-start.12
  252.4 1.7 copy-start.4
  257.0 7.0 copy-start.15
  257.7 455.7 %collective-permute-start.12 = (bf16[16,32,128]{2,1,0:T(8,128)(2,1)S(1)}, bf16[16,32,128]{2,1,0:T(8,128)(2,1)S(1)}, u32[]{:S(2)}, u32[]{:S(2)}) collective-permute-start(bf16[16,32,128]{2,1,0:T(8,128)(2,1)S(1)} %get-tuple-element.28), channel_id=1, source_target_pairs={{0,32},{32,64},{64,96},{96,128},{128,160},{160,192},{192,224},{224... | collective-permute-start | bytes 393224 | tf_op jit(solution)/shard_map/ppermute | solution.py:18
  262.0 451.4 %collective-permute-start.13 = (bf16[16,32,128]{2,1,0:T(8,128)(2,1)S(1)}, bf16[16,32,128]{2,1,0:T(8,128)(2,1)S(1)}, u32[]{:S(2)}, u32[]{:S(2)}) collective-permute-start(bf16[16,32,128]{2,1,0:T(8,128)(2,1)S(1)} %get-tuple-element.29), channel_id=1, source_target_pairs={{32,0},{64,32},{96,64},{128,96},{160,128},{192,160},{224,192},{256... | collective-permute-start | bytes 393224 | tf_op jit(solution)/shard_map/ppermute | solution.py:20
  264.0 449.6 %collective-permute-start.14 = (bf16[32,16,128]{2,1,0:T(8,128)(2,1)S(1)}, bf16[32,16,128]{2,1,0:T(8,128)(2,1)S(1)}, u32[]{:S(2)}, u32[]{:S(2)}) collective-permute-start(bf16[32,16,128]{2,1,0:T(8,128)(2,1)S(1)} %get-tuple-element.30), channel_id=1, source_target_pairs={{0,1},{1,2},{2,3},{3,4},{4,5},{5,6},{6,7},{7,8},{8,9},{9,10},{10,1... | collective-permute-start | bytes 393224 | tf_op jit(solution)/shard_map/ppermute | solution.py:18
  268.2 445.4 %collective-permute-start.15 = (bf16[32,16,128]{2,1,0:T(8,128)(2,1)S(1)}, bf16[32,16,128]{2,1,0:T(8,128)(2,1)S(1)}, u32[]{:S(2)}, u32[]{:S(2)}) collective-permute-start(bf16[32,16,128]{2,1,0:T(8,128)(2,1)S(1)} %get-tuple-element.31), channel_id=1, source_target_pairs={{1,0},{2,1},{3,2},{4,3},{5,4},{6,5},{7,6},{8,7},{9,8},{10,9},{11,1... | collective-permute-start | bytes 393224 | tf_op jit(solution)/shard_map/ppermute | solution.py:20
  (26 other events, 22.2 us)
Sparse Core Ops, SparseCore 0:
  257.8 453.8 all-reduce.6
where the time goes:
time: 724 us; the launch traced here: 723 us
  waiting for transfers between devices  466 us (64%)
  blocking collectives  141 us (19%)
  starting transfers between devices  46.6 us (6%)
  local copies, waits for them, and re-layouts  29.8 us (4%)
  matrix products  14.8 us (2%)
  between operations  14.8 us (2%)
  other arithmetic  10.1 us (1%)
    psum x1, waiting for transfers between devices, shards(): w_total, v_total = lax.psum((w_sum, v_sum), ('sta', 'src'))  442 us
    psum x1, blocking collectives, shards(): w_total, v_total = lax.psum((w_sum, v_sum), ('sta', 'src'))  115 us
    ppermute x8, starting transfers between devices, padded_2(): lax.ppermute(tail, axis, [(i, (i + 1) % count) for i in range(ends)])  30 us
    psum x1, blocking collectives, shards(): summed, count = lax.psum((partial_sum, local_count), 'sta')  25.8 us
    ppermute x8, starting transfers between devices, padded_2(): lax.ppermute(head, axis, [((i + 1) % count, i) for i in range(ends)])  16.6 us
    ppermute x8, waiting for transfers between devices, padded_2(): lax.ppermute(head, axis, [((i + 1) % count, i) for i in range(ends)])  15.3 us
  transfers between devices with their start and end apart: 17, of which 7 were waited for; matrix products, arithmetic and copies ran while one was open for 3% of the time, Pallas kernels for 0%

commit v1 on v0

--- a/solution.py
+++ b/solution.py
@@ -155,7 +155,7 @@
         from_src = from_src + jnp.pad(got_cols[:, 3 * HW :], ((0, 0), (src_rows - HW, 0), (0, 0)))
         grad = direct + from_sta + from_src
     w_sum = jnp.stack(w_rows[::-1])
-    w_total, v_total = lax.psum((w_sum, v_sum), ("sta", "src"))
+    w_total, v_total = lax.psum(lax.psum((w_sum, v_sum), "src"), "sta")
     node_total = jnp.float32(sta_rows * lax.axis_size("sta")) * jnp.float32(
         src_rows * lax.axis_size("src")
     )

time: 724 us -> 698 us (0.964)
  waiting for transfers between devices: 466 us -> 444 us
    psum x1 -> x2, waiting for transfers between devices: 442 us -> 420 us  [shards(): w_total, v_total = lax.psum(lax.psum((w_sum, v_sum), 'src'), 'sta')]
    psum x1 -> x2, blocking collectives: 115 us -> 113 us  [shards(): w_total, v_total = lax.psum(lax.psum((w_sum, v_sum), 'src'), 'sta')]
  transfers between devices with their start and end apart: 17 -> 18, of which waited for: 7 -> 9; matrix products, arithmetic and copies ran while one was open for 3% -> 3% of each run, Pallas kernels for 0% -> 0%
where the time goes in v1:
time: 698 us; the launch traced here: 697 us
  waiting for transfers between devices  444 us (64%)
  blocking collectives  139 us (20%)
  starting transfers between devices  43.9 us (6%)
  local copies, waits for them, and re-layouts  30 us (4%)
  matrix products  14.8 us (2%)
  between operations  14.8 us (2%)
  other arithmetic  10.1 us (1%)
    psum x2, waiting for transfers between devices, shards(): w_total, v_total = lax.psum(lax.psum((w_sum, v_sum), 'src'), 'sta')  420 us
    psum x2, blocking collectives, shards(): w_total, v_total = lax.psum(lax.psum((w_sum, v_sum), 'src'), 'sta')  113 us
    ppermute x8, starting transfers between devices, padded_2(): lax.ppermute(tail, axis, [(i, (i + 1) % count) for i in range(ends)])  26.8 us
    psum x1, blocking collectives, shards(): summed, count = lax.psum((partial_sum, local_count), 'sta')  25.8 us
    ppermute x8, starting transfers between devices, padded_2(): lax.ppermute(head, axis, [((i + 1) % count, i) for i in range(ends)])  17.1 us
    ppermute x8, waiting for transfers between devices, padded_2(): lax.ppermute(head, axis, [((i + 1) % count, i) for i in range(ends)])  15.5 us
  transfers between devices with their start and end apart: 18, of which 9 were waited for; matrix products, arithmetic and copies ran while one was open for 3% of the time, Pallas kernels for 0%

profile of v1, /device:TPU:1, one launch (start us, length us, event | category | flops | bytes accessed | tf_op | source)
XLA Modules:
  0.0 696.6 jit_solution(3448681736930924643)
XLA Ops:
  8.3 4.6 collective-permute-start
  12.9 5.5 collective-permute-start.1
  19.1 1.3 fusion.59
  20.5 1.3 fusion.60
  31.5 1.3 collective-permute-start.2
  32.8 1.3 collective-permute-start.3
  36.5 7.6 %collective-permute-done.2 = bf16[64,16,128]{2,0,1:T(8,128)(2,1)S(1)} collective-permute-done((bf16[64,16,128]{2,0,1:T(8,128)(2,1)S(1)}, bf16[64,16,128]{2,0,1:T(8,128)(2,1)S(1)}, u32[]{:S(2)}, u32[]{:S(2)}) %collective-permute-start.2) | collective-permute-done | bytes 262176 | tf_op jit(solution)/shard_map/ppermute | solution.py:18
  48.3 3.6 collective-permute-start.4
  51.9 1.9 collective-permute-start.5
  54.1 4.1 collective-permute-done.5
  58.3 5.6 collective-permute-start.6
  63.9 1.3 collective-permute-start.7
  67.5 5.6 collective-permute-done.7
  76.9 25.8 %all-reduce.4 = (f32[2,32]{1,0:T(2,128)S(1)}, f32[2]{0:T(128)S(1)}) all-reduce(f32[2,32]{1,0:T(2,128)S(1)} %bitcast.115, f32[2]{0:T(128)S(1)} %copy-done.40), channel_id=1, replica_groups=mesh['sta'=16,'src'=32] {'sta'}, use_global_device_ids=true, to_apply=%region_3.4 | all-reduce | flops 66 | bytes 528 | tf_op jit(solution)/shard_map/psum | solution.py:114
  105.1 1.2 mul.284
  108.8 1.4 copy.149
  110.8 2.4 fusion.69
  113.5 70.4 %psum.46 = f32[64]{0:T(128)S(1)} all-reduce(f32[64]{0:T(128)S(1)} %convolution_bitcast_fusion.9), channel_id=1, replica_groups=mesh['sta'=16,'src'=32] {'src'}, use_global_device_ids=true, to_apply=%region_8.9 | all-reduce | flops 64 | bytes 512 | tf_op jit(solution)/shard_map/psum | solution.py:158
  183.9 42.6 %psum.47 = f32[64]{0:T(128)S(1)} all-reduce(f32[64]{0:T(128)S(1)} %psum.46), channel_id=1, replica_groups=mesh['sta'=16,'src'=32] {'sta'}, use_global_device_ids=true, to_apply=%region_9.10 | all-reduce | flops 64 | bytes 512 | tf_op jit(solution)/shard_map/psum | solution.py:158
  229.2 2.1 collective-permute-start.8
  231.3 2.4 collective-permute-start.9
  233.7 2.9 collective-permute-start.10
  236.6 1.5 collective-permute-start.11
  239.8 5.6 collective-permute-done.11
  246.5 1.1 multiply_convert_fusion
  249.1 1.7 fusion.70
  255.1 3.1 collective-permute-start.12
  258.2 1.9 collective-permute-start.13
  260.8 3.6 collective-permute-start.14
  264.4 1.3 collective-permute-start.15
  265.7 275.6 %all-reduce.8.cloned.1.call-done = f32[2,3,64,64]{2,3,1,0:T(8,128)} async-done(((f32[2,3,64,64]{2,3,1,0:T(8,128)}), f32[2,3,64,64]{2,3,1,0:T(8,128)}) %all-reduce.8.cloned.1.call-update) | async-done | bytes 98320 | tf_op jit(solution)/shard_map/psum | solution.py:158
  543.8 144.2 %all-reduce.10.cloned.1.call-done = f32[2,3,64,64]{2,3,1,0:T(8,128)} async-done(((f32[2,3,64,64]{2,3,1,0:T(8,128)}), f32[2,3,64,64]{2,3,1,0:T(8,128)}) %all-reduce.10.cloned.1.call-update) | async-done | bytes 98320 | tf_op jit(solution)/shard_map/psum | solution.py:158
  (197 shorter events, 45.8 us)
Async XLA Ops:
  7.2 534.1 %all-reduce.8.cloned.1.call-start = ((), (), s32[]{:S(2)}) async-start(), calls=%async_computation | async-start | bytes 393216 | tf_op jit(solution)/shard_map/psum | solution.py:158
  8.3 23.0 %collective-permute-start = (bf16[16,32,128]{2,0,1:T(8,128)(2,1)S(1)}, bf16[16,32,128]{2,0,1:T(8,128)(2,1)S(1)}, u32[]{:S(2)}, u32[]{:S(2)}) collective-permute-start(bf16[16,32,128]{2,0,1:T(8,128)(2,1)S(1)} %copy.146), channel_id=1, source_target_pairs={{0,32},{32,64},{64,96},{96,128},{128,160},{160,192},{192,224},{224... | collective-permute-start | bytes 393224 | tf_op jit(solution)/shard_map/ppermute | solution.py:18
  12.9 9.9 %copy-start.19 = (bf16[2,3,64,64]{3,2,1,0:T(8,128)(2,1)S(1)}, bf16[2,3,64,64]{3,2,1,0:T(8,128)(2,1)}, u32[]{:S(2)}) copy-start(bf16[2,3,64,64]{3,2,1,0:T(8,128)(2,1)} %param.16) | copy-start | bytes 147460
  12.9 18.5 %collective-permute-start.1 = (bf16[16,32,128]{2,0,1:T(8,128)(2,1)S(1)}, bf16[16,32,128]{2,0,1:T(8,128)(2,1)S(1)}, u32[]{:S(2)}, u32[]{:S(2)}) collective-permute-start(bf16[16,32,128]{2,0,1:T(8,128)(2,1)S(1)} %copy.147), channel_id=1, source_target_pairs={{32,0},{64,32},{96,64},{128,96},{160,128},{192,160},{224,192},{256... | collective-permute-start | bytes 393224 | tf_op jit(solution)/shard_map/ppermute | solution.py:20
  19.1 57.0 %copy-start.20 = (f32[32,2]{0,1:T(2,128)}, f32[32,2]{0,1:T(2,128)S(1)}, u32[]{:S(2)}) copy-start(f32[32,2]{0,1:T(2,128)S(1)} %convert_bitcast_fusion) | copy-start | bytes 772
  22.8 1.5 copy-start
  24.3 40.9 %copy-start.22 = (bf16[32,64]{1,0:T(8,128)(2,1)}, bf16[32,64]{1,0:T(8,128)(2,1)S(1)}, u32[]{:S(2)}) copy-start(bf16[32,64]{1,0:T(8,128)(2,1)S(1)} %convert_reduce_fusion.1) | copy-start | bytes 12292
  31.5 12.6 %collective-permute-start.2 = (bf16[64,16,128]{2,0,1:T(8,128)(2,1)S(1)}, bf16[64,16,128]{2,0,1:T(8,128)(2,1)S(1)}, u32[]{:S(2)}, u32[]{:S(2)}) collective-permute-start(bf16[64,16,128]{2,0,1:T(8,128)(2,1)S(1)} %get-tuple-element.38), channel_id=1, source_target_pairs={{0,1},{1,2},{2,3},{3,4},{4,5},{5,6},{6,7},{7,8},{8,9},{9,10},{10,1... | collective-permute-start | bytes 786440 | tf_op jit(solution)/shard_map/ppermute | solution.py:18
  32.8 11.4 %collective-permute-start.3 = (bf16[64,16,128]{2,0,1:T(8,128)(2,1)S(1)}, bf16[64,16,128]{2,0,1:T(8,128)(2,1)S(1)}, u32[]{:S(2)}, u32[]{:S(2)}) collective-permute-start(bf16[64,16,128]{2,0,1:T(8,128)(2,1)S(1)} %get-tuple-element.39), channel_id=1, source_target_pairs={{1,0},{2,1},{3,2},{4,3},{5,4},{6,5},{7,6},{8,7},{9,8},{10,9},{11,1... | collective-permute-start | bytes 786440 | tf_op jit(solution)/shard_map/ppermute | solution.py:20
  36.5 7.8 %copy-start.25 = (bf16[32,64]{1,0:T(8,128)(2,1)S(1)}, bf16[32,64]{1,0:T(8,128)(2,1)}, u32[]{:S(2)}) copy-start(bf16[32,64]{1,0:T(8,128)(2,1)} %convert_reduce_fusion) | copy-start | bytes 12292
  48.3 5.7 collective-permute-start.4
  51.9 6.3 collective-permute-start.5
  58.3 6.9 copy-start.37
  58.3 9.1 %collective-permute-start.6 = (bf16[64,16,128]{2,1,0:T(8,128)(2,1)S(1)}, bf16[64,16,128]{2,1,0:T(8,128)(2,1)S(1)}, u32[]{:S(2)}, u32[]{:S(2)}) collective-permute-start(bf16[64,16,128]{2,1,0:T(8,128)(2,1)S(1)} %get-tuple-element.36), channel_id=1, source_target_pairs={{0,1},{1,2},{2,3},{3,4},{4,5},{5,6},{6,7},{7,8},{8,9},{9,10},{10,1... | collective-permute-start | bytes 786440 | tf_op jit(solution)/shard_map/ppermute | solution.py:18
  63.9 9.1 %collective-permute-start.7 = (bf16[64,16,128]{2,1,0:T(8,128)(2,1)S(1)}, bf16[64,16,128]{2,1,0:T(8,128)(2,1)S(1)}, u32[]{:S(2)}, u32[]{:S(2)}) collective-permute-start(bf16[64,16,128]{2,1,0:T(8,128)(2,1)S(1)} %get-tuple-element.37), channel_id=1, source_target_pairs={{1,0},{2,1},{3,2},{4,3},{5,4},{6,5},{7,6},{8,7},{9,8},{10,9},{11,1... | collective-permute-start | bytes 786440 | tf_op jit(solution)/shard_map/ppermute | solution.py:20
  66.7 6.4 copy-start.26
  110.8 2.5 copy-start.1
  113.2 113.9 %copy-start.7 = (bf16[2048,64]{1,0:T(8,128)(2,1)S(1)}, bf16[2048,64]{1,0:T(8,128)(2,1)}, u32[]{:S(2)}) copy-start(bf16[2048,64]{1,0:T(8,128)(2,1)} %reshape.269) | copy-start | bytes 786436
  228.1 5.5 copy-start.16
  229.2 8.9 %copy-start.5 = (bf16[2048,64]{1,0:T(8,128)(2,1)S(1)}, bf16[2048,64]{1,0:T(8,128)(2,1)}, u32[]{:S(2)}) copy-start(bf16[2048,64]{1,0:T(8,128)(2,1)} %reshape.266) | copy-start | bytes 786436
  229.2 9.8 %collective-permute-start.8 = (bf16[16,32,128]{2,1,0:T(8,128)(2,1)S(1)}, bf16[16,32,128]{2,1,0:T(8,128)(2,1)S(1)}, u32[]{:S(2)}, u32[]{:S(2)}) collective-permute-start(bf16[16,32,128]{2,1,0:T(8,128)(2,1)S(1)} %get-tuple-element.32), channel_id=1, source_target_pairs={{0,32},{32,64},{64,96},{96,128},{128,160},{160,192},{192,224},{224... | collective-permute-start | bytes 393224 | tf_op jit(solution)/shard_map/ppermute | solution.py:18
  231.3 7.8 %collective-permute-start.9 = (bf16[16,32,128]{2,1,0:T(8,128)(2,1)S(1)}, bf16[16,32,128]{2,1,0:T(8,128)(2,1)S(1)}, u32[]{:S(2)}, u32[]{:S(2)}) collective-permute-start(bf16[16,32,128]{2,1,0:T(8,128)(2,1)S(1)} %get-tuple-element.33), channel_id=1, source_target_pairs={{32,0},{64,32},{96,64},{128,96},{160,128},{192,160},{224,192},{256... | collective-permute-start | bytes 393224 | tf_op jit(solution)/shard_map/ppermute | solution.py:20
  233.7 6.1 collective-permute-start.10
  236.6 8.8 %collective-permute-start.11 = (bf16[32,16,128]{2,1,0:T(8,128)(2,1)S(1)}, bf16[32,16,128]{2,1,0:T(8,128)(2,1)S(1)}, u32[]{:S(2)}, u32[]{:S(2)}) collective-permute-start(bf16[32,16,128]{2,1,0:T(8,128)(2,1)S(1)} %get-tuple-element.35), channel_id=1, source_target_pairs={{1,0},{2,1},{3,2},{4,3},{5,4},{6,5},{7,6},{8,7},{9,8},{10,9},{11,1... | collective-permute-start | bytes 393224 | tf_op jit(solution)/shard_map/ppermute | solution.py:20
  239.2 6.4 copy-start.12
  249.1 1.7 copy-start.4
  254.4 433.7 %all-reduce.10.cloned.1.call-start = ((), (), s32[]{:S(2)}) async-start(), calls=%async_computation.1 | async-start | bytes 393216 | tf_op jit(solution)/shard_map/psum | solution.py:158
  255.0 5.1 copy-start.15
  255.1 286.3 %collective-permute-start.12 = (bf16[16,32,128]{2,1,0:T(8,128)(2,1)S(1)}, bf16[16,32,128]{2,1,0:T(8,128)(2,1)S(1)}, u32[]{:S(2)}, u32[]{:S(2)}) collective-permute-start(bf16[16,32,128]{2,1,0:T(8,128)(2,1)S(1)} %get-tuple-element.28), channel_id=1, source_target_pairs={{0,32},{32,64},{64,96},{96,128},{128,160},{160,192},{192,224},{224... | collective-permute-start | bytes 393224 | tf_op jit(solution)/shard_map/ppermute | solution.py:18
  258.2 283.1 %collective-permute-start.13 = (bf16[16,32,128]{2,1,0:T(8,128)(2,1)S(1)}, bf16[16,32,128]{2,1,0:T(8,128)(2,1)S(1)}, u32[]{:S(2)}, u32[]{:S(2)}) collective-permute-start(bf16[16,32,128]{2,1,0:T(8,128)(2,1)S(1)} %get-tuple-element.29), channel_id=1, source_target_pairs={{32,0},{64,32},{96,64},{128,96},{160,128},{192,160},{224,192},{256... | collective-permute-start | bytes 393224 | tf_op jit(solution)/shard_map/ppermute | solution.py:20
  260.8 280.7 %collective-permute-start.14 = (bf16[32,16,128]{2,1,0:T(8,128)(2,1)S(1)}, bf16[32,16,128]{2,1,0:T(8,128)(2,1)S(1)}, u32[]{:S(2)}, u32[]{:S(2)}) collective-permute-start(bf16[32,16,128]{2,1,0:T(8,128)(2,1)S(1)} %get-tuple-element.30), channel_id=1, source_target_pairs={{0,1},{1,2},{2,3},{3,4},{4,5},{5,6},{6,7},{7,8},{8,9},{9,10},{10,1... | collective-permute-start | bytes 393224 | tf_op jit(solution)/shard_map/ppermute | solution.py:18
  264.4 277.1 %collective-permute-start.15 = (bf16[32,16,128]{2,1,0:T(8,128)(2,1)S(1)}, bf16[32,16,128]{2,1,0:T(8,128)(2,1)S(1)}, u32[]{:S(2)}, u32[]{:S(2)}) collective-permute-start(bf16[32,16,128]{2,1,0:T(8,128)(2,1)S(1)} %get-tuple-element.31), channel_id=1, source_target_pairs={{1,0},{2,1},{3,2},{4,3},{5,4},{6,5},{7,6},{8,7},{9,8},{10,9},{11,1... | collective-permute-start | bytes 393224 | tf_op jit(solution)/shard_map/ppermute | solution.py:20
  (27 other events, 23.5 us)
Sparse Core Ops, SparseCore 0:
  254.5 286.7 all-reduce.7
  544.5 143.5 all-reduce.9
